TPU v7x, 512 devices: a whole 4x4x16 slice. The times are simulated.
512 devices in a mesh: ctx: 64 (over z, y), head: 8 (over x, core).
Axes of the slice: x: 4, y: 4, z: 16, core: 2. Of those that a mesh axis runs over, the one named last changes fastest.
Arguments:
- query_lin: bfloat16 [8192, 256], P('ctx', 'head'), may hold values from -4 to 4
- key_lin: bfloat16 [8192, 256], P('ctx', 'head'), may hold values from -4 to 4
- values: bfloat16 [8192, 2048], P('ctx', 'head'), may hold values from -24 to 24
- win_queries: bfloat16 [8192, 2048], P('ctx', 'head'), may hold values from -6 to 6
- win_keys: bfloat16 [8192, 2048], P('ctx', 'head'), may hold values from -6 to 6
- gain: float32 [2048], P('head'), may hold values from 0.1 to 1.9
- grad_out: bfloat16 [8192, 2048], P('ctx', 'head'), may hold values from -6 to 6
Outputs:
- mixed_out: bfloat16 [8192, 2048], P('ctx', 'head')
- grad_query_lin: bfloat16 [8192, 256], P('ctx', 'head')
- grad_key_lin: bfloat16 [8192, 256], P('ctx', 'head')
- grad_values: bfloat16 [8192, 2048], P('ctx', 'head')
- grad_win_queries: bfloat16 [8192, 2048], P('ctx', 'head')
- grad_win_keys: bfloat16 [8192, 2048], P('ctx', 'head')
All inputs are finite; a program needn't handle non-finite values.
Results may differ from a plain program's by a relative error of at most 0.015.
Values may be sent and summed in bfloat16 or wider, within the bound.
A program may use at most 128 MiB of HBM per device.

v0:
```python
import math
import jax
import jax.numpy as jnp
from jax import lax
from jax.sharding import PartitionSpec as P

HEADS = 16
KD = 16
DV = 128
WD = 128
WINDOW = 128
epsilon = 1e-06


def from_behind(value, axis, by):
    size = lax.axis_size(axis)
    pairs = [(i, i + by) for i in range(size) if 0 <= i + by < size]
    return lax.ppermute(value, axis, pairs)


def prefix_2(value, axis, join, neutral, backward):
    count = lax.axis_size(axis)
    place = lax.axis_index(axis)
    ahead = count - 1 - place if backward else place
    gathered = lax.all_gather(value.astype(jnp.bfloat16), axis)
    state = jnp.zeros_like(value) + jnp.asarray(neutral, value.dtype)

    def one(step, state):
        source = count - 1 - step if backward else step
        return join(state, lax.dynamic_index_in_dim(gathered, source, 0, False).astype(value.dtype))

    return lax.fori_loop(0, ahead, one, state)


def features_cols(points):
    head_count = points.shape[0]
    key_depth = points.shape[1]
    tok_count = points.shape[2]
    linear_part = points / math.sqrt(math.sqrt(key_depth))
    outer_part = (points[:, :, None, :] * points[:, None, :, :]).reshape(
        head_count, key_depth * key_depth, tok_count
    )
    outer_part = outer_part / (math.sqrt(2.0) * math.sqrt(key_depth))
    return jnp.concatenate([jnp.ones_like(points[:, :1, :]), linear_part, outer_part], axis=1)


def accumulate(earlier, upcoming):
    return earlier + upcoming


def window_math(query_blocks, key_pairs, value_pairs, dout_blocks, allowed, scale_win):
    scores = (
        jnp.einsum("bthe,bshe->bhts", query_blocks, key_pairs, preferred_element_type=jnp.float32)
        * scale_win
    )
    row_top = jnp.max(jnp.where(allowed, scores, -jnp.inf), axis=-1, keepdims=True)
    weights = jnp.where(allowed, jnp.exp(scores - row_top), 0.0)
    row_total = jnp.sum(weights, axis=-1, keepdims=True)
    soft_probs = weights / row_total
    probs_round = soft_probs.astype(jnp.bfloat16)
    win_out = jnp.einsum(
        "bhts,bshd->bthd", probs_round, value_pairs, preferred_element_type=jnp.float32
    )
    grad_prob = jnp.einsum(
        "bthd,bshd->bhts", dout_blocks, value_pairs, preferred_element_type=jnp.float32
    )
    row_delta = jnp.transpose(
        jnp.sum(dout_blocks.astype(jnp.float32) * win_out, axis=-1), (0, 2, 1)
    )[..., None]
    grad_score = (soft_probs * (grad_prob - row_delta)).astype(jnp.bfloat16)
    grad_query = (
        jnp.einsum("bhts,bshe->bthe", grad_score, key_pairs, preferred_element_type=jnp.float32)
        * scale_win
    )
    grad_keys = (
        jnp.einsum("bhts,bthe->bshe", grad_score, query_blocks, preferred_element_type=jnp.float32)
        * scale_win
    )
    grad_vals = jnp.einsum(
        "bhts,bthd->bshd", probs_round, dout_blocks, preferred_element_type=jnp.float32
    )
    return (win_out, grad_query, grad_keys, grad_vals, row_top, row_total, row_delta)


def shards(query_lin, key_lin, values, win_queries, win_keys, gain, grad_out):
    tok_rows = query_lin.shape[0]
    head_count = values.shape[1] // DV
    full_width = HEADS * DV
    scale_lin = 1.0 / math.sqrt(KD)
    scale_win = 1.0 / math.sqrt(WD)
    ctx_index = lax.axis_index("ctx")
    tail_start = tok_rows - WINDOW
    rim_keys, rim_values = from_behind((win_keys, values), "ctx", 1)
    query_h = query_lin.reshape(tok_rows, head_count, KD)
    key_h = key_lin.reshape(tok_rows, head_count, KD)
    value_h = values.reshape(tok_rows, head_count, DV)
    query_cols = jnp.transpose(query_h, (1, 2, 0)).astype(jnp.float32)
    key_cols = jnp.transpose(key_h, (1, 2, 0)).astype(jnp.float32)
    query_feat, pull_query = jax.vjp(features_cols, query_cols)
    key_feat, pull_key = jax.vjp(features_cols, key_cols)
    query_phi = query_feat.astype(jnp.bfloat16)
    key_phi = key_feat.astype(jnp.bfloat16)
    local_state = jnp.einsum("hfs,shd->hfd", key_phi, value_h, preferred_element_type=jnp.float32)
    state_zero = jnp.zeros_like(local_state)
    prefix = prefix_2(local_state, "ctx", accumulate, state_zero, False)
    prefix_round = prefix.astype(jnp.bfloat16)
    lin_score = (
        jnp.einsum("thk,shk->hts", query_h, key_h, preferred_element_type=jnp.float32) * scale_lin
    )
    causal = jnp.tril(jnp.ones((tok_rows, tok_rows), jnp.bool_))
    kernel = jnp.where(causal, 1.0 + lin_score + 0.5 * lin_score * lin_score, 0.0).astype(
        jnp.bfloat16
    )
    linear_out = jnp.einsum("hts,shd->thd", kernel, value_h, preferred_element_type=jnp.float32)
    linear_out = linear_out + jnp.einsum(
        "hft,hfd->thd", query_phi, prefix_round, preferred_element_type=jnp.float32
    )
    linear_flat = linear_out.reshape(tok_rows, head_count * DV)
    dout_f = grad_out.astype(jnp.float32)
    square_sum = lax.psum(jnp.sum(linear_flat * linear_flat, axis=1), "head")
    inverse = (1.0 / jnp.sqrt(square_sum / full_width + epsilon))[:, None]
    blocks = tok_rows // WINDOW
    keys_ext = jnp.concatenate([rim_keys, win_keys], axis=0).reshape(
        blocks + 1, WINDOW, head_count, WD
    )
    values_ext = jnp.concatenate([rim_values, values], axis=0).reshape(
        blocks + 1, WINDOW, head_count, DV
    )
    key_pairs = jnp.concatenate([keys_ext[:-1], keys_ext[1:]], axis=1)
    value_pairs = jnp.concatenate([values_ext[:-1], values_ext[1:]], axis=1)
    query_blocks = win_queries.reshape(blocks, WINDOW, head_count, WD)
    dout_blocks = grad_out.reshape(blocks, WINDOW, head_count, DV)
    row_pos = jnp.arange(WINDOW, dtype=jnp.int32)[:, None]
    col_pos = jnp.arange(2 * WINDOW, dtype=jnp.int32)[None, :]
    band_mask = (col_pos > row_pos) & (col_pos <= row_pos + WINDOW)
    key_start = (
        ctx_index * tok_rows
        + jnp.arange(blocks, dtype=jnp.int32)[:, None, None] * WINDOW
        - WINDOW
        + col_pos[None]
    )
    allowed = (band_mask[None] & (key_start >= 0))[:, None]
    win_out, grad_wq, key_grads, value_grads, row_top, row_total, row_delta = window_math(
        query_blocks, key_pairs, value_pairs, dout_blocks, allowed, scale_win
    )
    window_flat = win_out.reshape(tok_rows, head_count * DV)
    mixed_out = (linear_flat * inverse * gain + window_flat).astype(jnp.bfloat16)
    cross_sum = lax.psum(jnp.sum(gain * dout_f * linear_flat, axis=1), "head")
    grad_lin = (
        inverse * gain * dout_f
        - linear_flat * inverse * inverse * inverse * (cross_sum / full_width)[:, None]
    ).astype(jnp.bfloat16)
    grad_lin_h = grad_lin.reshape(tok_rows, head_count, DV)
    value_dot = jnp.einsum("thd,shd->hts", grad_lin_h, value_h, preferred_element_type=jnp.float32)
    grad_score = jnp.where(causal, value_dot * (1.0 + lin_score), 0.0).astype(jnp.bfloat16)
    query_pull = jnp.einsum(
        "thd,hfd->hft", grad_lin_h, prefix_round, preferred_element_type=jnp.float32
    )
    grad_query = (
        jnp.einsum("hts,shk->thk", grad_score, key_h, preferred_element_type=jnp.float32)
        * scale_lin
    )
    grad_query = grad_query + jnp.transpose(pull_query(query_pull)[0], (2, 0, 1))
    local_back = jnp.einsum(
        "hft,thd->hfd", query_phi, grad_lin_h, preferred_element_type=jnp.float32
    )
    suffix = prefix_2(local_back, "ctx", accumulate, state_zero, True)
    suffix_round = suffix.astype(jnp.bfloat16)
    grad_value_lin = jnp.einsum(
        "hts,thd->shd", kernel, grad_lin_h, preferred_element_type=jnp.float32
    )
    grad_value_lin = grad_value_lin + jnp.einsum(
        "hfs,hfd->shd", key_phi, suffix_round, preferred_element_type=jnp.float32
    )
    key_pull = jnp.einsum("shd,hfd->hfs", value_h, suffix_round, preferred_element_type=jnp.float32)
    grad_key = (
        jnp.einsum("hts,thk->shk", grad_score, query_h, preferred_element_type=jnp.float32)
        * scale_lin
    )
    grad_key = grad_key + jnp.transpose(pull_key(key_pull)[0], (2, 0, 1))
    pad_tail = ((0, 1), (0, 0), (0, 0), (0, 0))
    pad_head = ((1, 0), (0, 0), (0, 0), (0, 0))
    key_ext_grad = jnp.pad(key_grads[:, :WINDOW], pad_tail) + jnp.pad(
        key_grads[:, WINDOW:], pad_head
    )
    value_ext_grad = jnp.pad(value_grads[:, :WINDOW], pad_tail) + jnp.pad(
        value_grads[:, WINDOW:], pad_head
    )
    key_own = key_ext_grad[1:].reshape(tok_rows, head_count * WD)
    value_own = value_ext_grad[1:].reshape(tok_rows, head_count * DV)
    back_keys, back_values = (
        from_behind(
            key_ext_grad[0].reshape(WINDOW, head_count * WD).astype(jnp.bfloat16), "ctx", -1
        ).astype(jnp.float32),
        from_behind(
            value_ext_grad[0].reshape(WINDOW, head_count * DV).astype(jnp.bfloat16), "ctx", -1
        ).astype(jnp.float32),
    )
    key_own = jnp.concatenate([key_own[:tail_start], key_own + back_keys], axis=0)
    value_own = jnp.concatenate([value_own[:tail_start], value_own + back_values], axis=0)
    grad_query_lin = grad_query.astype(jnp.bfloat16).reshape(tok_rows, head_count * KD)
    grad_key_lin = grad_key.astype(jnp.bfloat16).reshape(tok_rows, head_count * KD)
    grad_values = (grad_value_lin.reshape(tok_rows, head_count * DV) + value_own).astype(
        jnp.bfloat16
    )
    grad_win_queries = grad_wq.reshape(tok_rows, head_count * WD).astype(jnp.bfloat16)
    grad_win_keys = key_own.astype(jnp.bfloat16)
    return (mixed_out, grad_query_lin, grad_key_lin, grad_values, grad_win_queries, grad_win_keys)


def solution(mesh):
    placed = (
        P("ctx", "head"),
        P("ctx", "head"),
        P("ctx", "head"),
        P("ctx", "head"),
        P("ctx", "head"),
        P("head"),
        P("ctx", "head"),
    )
    return jax.shard_map(
        shards,
        mesh=mesh,
        in_specs=placed,
        out_specs=(
            P("ctx", "head"),
            P("ctx", "head"),
            P("ctx", "head"),
            P("ctx", "head"),
            P("ctx", "head"),
            P("ctx", "head"),
        ),
        check_vma=False,
    )
```

profile of v0, /device:TPU:2, one launch (start us, length us, event | category | flops | bytes accessed | tf_op | source)
XLA Modules:
  0.0 470.7 jit_solution(8082545731358047730)
XLA Ops:
  8.7 1.8 convolution_convert_fusion.1
  10.6 3.5 collective-permute-start
  15.0 3.5 collective-permute-start.1
  19.6 1.0 copy.121
  25.0 150.1 %all-gather.5.cloned.1.call-done = bf16[128,273,128]{2,1,0:T(8,128)(2,1)} async-done(((bf16[2,273,128]{2,1,0:T(8,128)(2,1)}), bf16[128,273,128]{2,1,0:T(8,128)(2,1)}) %all-gather.5.cloned.1.call-update) | async-done | bytes 8945680 | tf_op jit(solution)/shard_map/all_gather | solution.py:25
  176.0 10.0 %all-reduce.4 = (f32[128]{0:T(128)S(1)}, f32[128]{0:T(128)S(1)}) all-reduce(f32[128]{0:T(128)S(1)} %get-tuple-element.137, f32[128]{0:T(128)S(1)} %multiply_reduce_fusion.4), channel_id=1, replica_groups=mesh['ctx'=64,'head'=8] {'head'}, use_global_device_ids=true, to_apply=%region_3.4 | all-reduce | flops 256 | bytes 2048 | tf_op jit(solution)/shard_map/psum | solution.py:120
  186.9 1.0 convolution_convert_fusion
  189.5 1.3 collective-permute-start.3
  191.3 1.3 collective-permute-start.2
  192.7 2.9 collective-permute-done.3
  197.7 202.1 %all-gather.7.cloned.1.call-done = bf16[128,273,128]{2,1,0:T(8,128)(2,1)} async-done(((bf16[2,273,128]{2,1,0:T(8,128)(2,1)}), bf16[128,273,128]{2,1,0:T(8,128)(2,1)}) %all-gather.7.cloned.1.call-update) | async-done | bytes 8945680 | tf_op jit(solution)/shard_map/all_gather | solution.py:25
  399.9 61.5 %while.23 = (s32[]{:T(128)}, f32[2,273,128]{2,1,0:T(8,128)S(1)}, s32[]{:T(128)}, bf16[64,2,273,128]{3,2,1,0:T(8,128)(2,1)}, s32[]{:T(128)}, /*index=5*/s32[]{:T(128)}, s32[]{:T(128)}, s32[]{:T(128)}) while((s32[]{:T(128)}, f32[2,273,128]{2,1,0:T(8,128)S(1)}, s32[]{:T(128)}, bf16[64,2,273,128]{3,2,1,0:T(8,128)(2,1)}, s32[]{:T(128)}, ...), condition=%wide.region_11.12_spmd, body=%wide.region_10.11_spmd.sunk | while | flops 139782 | bytes 699023 | solution.py:32
  399.9 1.0 convert_add_fusion.5
  400.9 1.0 convert_add_fusion.5
  401.9 1.0 convert_add_fusion.5
  402.8 1.0 convert_add_fusion.5
  403.8 1.0 convert_add_fusion.5
  404.8 1.0 convert_add_fusion.5
  405.8 1.0 convert_add_fusion.5
  406.7 1.0 convert_add_fusion.5
  407.7 1.0 convert_add_fusion.5
  408.7 1.0 convert_add_fusion.5
  409.7 1.0 convert_add_fusion.5
  410.6 1.0 convert_add_fusion.5
  411.6 1.0 convert_add_fusion.5
  412.6 1.0 convert_add_fusion.5
  413.6 1.0 convert_add_fusion.5
  414.6 1.0 convert_add_fusion.5
  415.5 1.0 convert_add_fusion.5
  416.5 1.0 convert_add_fusion.5
  417.5 1.0 convert_add_fusion.5
  418.5 1.0 convert_add_fusion.5
  419.4 1.0 convert_add_fusion.5
  420.4 1.0 convert_add_fusion.5
  421.4 1.0 convert_add_fusion.5
  422.4 1.0 convert_add_fusion.5
  423.3 1.0 convert_add_fusion.5
  424.3 1.0 convert_add_fusion.5
  425.3 1.0 convert_add_fusion.5
  426.3 1.0 convert_add_fusion.5
  427.3 1.0 convert_add_fusion.5
  428.2 1.0 convert_add_fusion.5
  429.2 1.0 convert_add_fusion.5
  430.2 1.0 convert_add_fusion.5
  431.2 1.0 convert_add_fusion.5
  432.1 1.0 convert_add_fusion.5
  433.1 1.0 convert_add_fusion.5
  434.1 1.0 convert_add_fusion.5
  435.1 1.0 convert_add_fusion.5
  436.0 1.0 convert_add_fusion.5
  437.0 1.0 convert_add_fusion.5
  438.0 1.0 convert_add_fusion.5
  440.9 1.0 convert_add_fusion.5
  441.9 1.0 convert_add_fusion.5
  442.9 1.0 convert_add_fusion.5
  443.9 1.0 convert_add_fusion.5
  444.8 1.0 convert_add_fusion.5
  449.7 1.0 convert_add_fusion.5
  450.7 1.0 convert_add_fusion.5
  451.7 1.0 convert_add_fusion.5
  452.7 1.0 convert_add_fusion.5
  453.6 1.0 convert_add_fusion.5
  459.5 1.0 convert_add_fusion.5
  460.5 1.0 convert_add_fusion.5
  (88 shorter events, 26.8 us)
Async XLA Ops:
  7.2 168.3 %copy-start = (bf16[128,256]{1,0:T(8,128)(2,1)S(1)}, bf16[128,256]{1,0:T(8,128)(2,1)}, u32[]{:S(2)}) copy-start(bf16[128,256]{1,0:T(8,128)(2,1)} %param.13) | copy-start | bytes 196612
  7.2 168.7 %copy-start.1 = (bf16[128,256]{1,0:T(8,128)(2,1)S(1)}, bf16[128,256]{1,0:T(8,128)(2,1)}, u32[]{:S(2)}) copy-start(bf16[128,256]{1,0:T(8,128)(2,1)} %param.17) | copy-start | bytes 196612
  7.2 168.7 %copy-start.4 = (f32[256]{0:T(256)S(1)}, f32[256]{0:T(256)}, u32[]{:S(2)}) copy-start(f32[256]{0:T(256)} %param.16) | copy-start | bytes 3076
  7.2 167.9 %all-gather.5.cloned.1.call-start = ((), (), s32[]{:S(2)}) async-start(), calls=%async_computation | async-start | bytes 9318400 | tf_op jit(solution)/shard_map/all_gather | solution.py:25
  10.5 389.3 %all-gather.7.cloned.1.call-start = ((), (), s32[]{:S(2)}) async-start(), calls=%async_computation.1 | async-start | bytes 9318400 | tf_op jit(solution)/shard_map/all_gather | solution.py:25
  10.6 13.6 %collective-permute-start = (bf16[128,256]{1,0:T(8,128)(2,1)}, bf16[128,256]{1,0:T(8,128)(2,1)S(1)}, u32[]{:S(2)}, u32[]{:S(2)}) collective-permute-start(bf16[128,256]{1,0:T(8,128)(2,1)} %param.13), channel_id=1, source_target_pairs={{0,8},{8,16},{16,24},{24,32},{32,40},{40,48},{48,56},{56,64},{64,7... | collective-permute-start | bytes 196616 | tf_op jit(solution)/shard_map/ppermute | solution.py:18
  15.0 9.0 %collective-permute-start.1 = (bf16[128,256]{0,1:T(8,128)(2,1)S(1)}, bf16[128,256]{0,1:T(8,128)(2,1)S(1)}, u32[]{:S(2)}, u32[]{:S(2)}) collective-permute-start(bf16[128,256]{0,1:T(8,128)(2,1)S(1)} %copy.83), channel_id=1, source_target_pairs={{0,8},{8,16},{16,24},{24,32},{32,40},{40,48},{48,56},{56,64},{64,7... | collective-permute-start | bytes 196616 | tf_op jit(solution)/shard_map/ppermute | solution.py:18
  24.3 172.7 %copy-start.2 = (bf16[128,32]{0,1:T(8,128)(2,1)S(1)}, bf16[128,32]{0,1:T(8,128)(2,1)}, u32[]{:S(2)}) copy-start(bf16[128,32]{0,1:T(8,128)(2,1)} %param.12) | copy-start | bytes 24580
  175.1 287.2 %copy-start.3 = (bf16[128,32]{0,1:T(8,128)(2,1)S(1)}, bf16[128,32]{0,1:T(8,128)(2,1)}, u32[]{:S(2)}) copy-start(bf16[128,32]{0,1:T(8,128)(2,1)} %param.11) | copy-start | bytes 24580
  189.5 6.2 %collective-permute-start.3 = (bf16[128,256]{0,1:T(8,128)(2,1)S(1)}, bf16[128,256]{0,1:T(8,128)(2,1)S(1)}, u32[]{:S(2)}, u32[]{:S(2)}) collective-permute-start(bf16[128,256]{0,1:T(8,128)(2,1)S(1)} %bitcast.205), channel_id=1, source_target_pairs={{8,0},{16,8},{24,16},{32,24},{40,32},{48,40},{56,48},{64,56},{72,6... | collective-permute-start | bytes 196616 | tf_op jit(solution)/shard_map/ppermute | solution.py:18
  191.3 271.9 %collective-permute-start.2 = (bf16[128,256]{1,0:T(8,128)(2,1)S(1)}, bf16[128,256]{1,0:T(8,128)(2,1)S(1)}, u32[]{:S(2)}, u32[]{:S(2)}) collective-permute-start(bf16[128,256]{1,0:T(8,128)(2,1)S(1)} %copy.99), channel_id=1, source_target_pairs={{8,0},{16,8},{24,16},{32,24},{40,32},{48,40},{56,48},{64,56},{72,6... | collective-permute-start | bytes 196616 | tf_op jit(solution)/shard_map/ppermute | solution.py:18
Sparse Core Ops, SparseCore 0:
  11.0 164.0 all-gather.4
  188.0 211.8 all-gather.6
where the time goes:
time: 473 us; the launch traced here: 471 us
  waiting for transfers between devices  355 us (75%)
  other arithmetic  65.1 us (14%)
  between operations  14.5 us (3%)
  blocking collectives  10 us (2%)
  starting transfers between devices  9.63 us (2%)
  matrix products  8.27 us (2%)
  local copies, waits for them, and re-layouts  6.56 us (1%)
    all_gather x2, waiting for transfers between devices, prefix_2(): gathered = lax.all_gather(value.astype(jnp.bfloat16), axis)  352 us
    add x63, other arithmetic, accumulate(): return earlier + upcoming  60.1 us
    psum x1, blocking collectives, shards(): square_sum = lax.psum(jnp.sum(linear_flat * linear_flat, axis=1), 'head')  10 us
    ppermute x4, starting transfers between devices, from_behind(): return lax.ppermute(value, axis, pairs)  9.55 us
  transfers between devices with their start and end apart: 6, of which 3 were waited for; matrix products, arithmetic and copies ran while one was open for 16% of the time, Pallas kernels for 0%

commit v1 on v0

--- a/solution.py
+++ b/solution.py
@@ -117,7 +117,12 @@
     )
     linear_flat = linear_out.reshape(tok_rows, head_count * DV)
     dout_f = grad_out.astype(jnp.float32)
-    square_sum = lax.psum(jnp.sum(linear_flat * linear_flat, axis=1), "head")
+
+    def ports_bring(payload):
+        outcome_arr = jnp.sum(lax.all_gather(payload, "head"), 0)
+        return outcome_arr
+
+    square_sum = ports_bring(jnp.sum(linear_flat * linear_flat, axis=1))
     inverse = (1.0 / jnp.sqrt(square_sum / full_width + epsilon))[:, None]
     blocks = tok_rows // WINDOW
     keys_ext = jnp.concatenate([rim_keys, win_keys], axis=0).reshape(

time: 473 us -> 482 us (1.019)
  blocking collectives: 10 us -> 20.7 us
    all_gather x0 -> x1, blocking collectives: none -> 10.7 us  [ports_bring(): outcome_arr = jnp.sum(lax.all_gather(payload, 'head'), 0)]
  transfers between devices with their start and end apart: 6 -> 6, of which waited for: 3 -> 3; matrix products, arithmetic and copies ran while one was open for 16% -> 15% of each run, Pallas kernels for 0% -> 0%
where the time goes in v1:
time: 482 us; the launch traced here: 480 us
  waiting for transfers between devices  353 us (73%)
  other arithmetic  65.1 us (14%)
  blocking collectives  20.7 us (4%)
  between operations  14.5 us (3%)
  starting transfers between devices  9.63 us (2%)
  matrix products  8.27 us (2%)
  local copies, waits for them, and re-layouts  6.56 us (1%)
    all_gather x2, waiting for transfers between devices, prefix_2(): gathered = lax.all_gather(value.astype(jnp.bfloat16), axis)  350 us
    add x63, other arithmetic, accumulate(): return earlier + upcoming  60.1 us
    all_gather x1, blocking collectives, ports_bring(): outcome_arr = jnp.sum(lax.all_gather(payload, 'head'), 0)  10.7 us
    psum x1, blocking collectives, shards(): cross_sum = lax.psum(jnp.sum(gain * dout_f * linear_flat, axis=1), 'head')  10 us
  transfers between devices with their start and end apart: 6, of which 3 were waited for; matrix products, arithmetic and copies ran while one was open for 15% of the time, Pallas kernels for 0%

profile of v1, /device:TPU:2, one launch (start us, length us, event | category | flops | bytes accessed | tf_op | source)
XLA Modules:
  0.0 479.6 jit_solution(8096287302822193234)
XLA Ops:
  8.7 1.8 convolution_convert_fusion.1
  10.6 3.5 collective-permute-start
  15.0 3.5 collective-permute-start.1
  19.6 1.0 copy.121
  25.0 150.1 %all-gather.7.cloned.1.call-done = bf16[128,273,128]{2,1,0:T(8,128)(2,1)} async-done(((bf16[2,273,128]{2,1,0:T(8,128)(2,1)}), bf16[128,273,128]{2,1,0:T(8,128)(2,1)}) %all-gather.7.cloned.1.call-update) | async-done | bytes 8945680 | tf_op jit(solution)/shard_map/all_gather | solution.py:25
  176.0 10.0 %psum.7 = f32[128]{0:T(128)S(1)} all-reduce(f32[128]{0:T(128)S(1)} %multiply_reduce_fusion.4), channel_id=1, replica_groups=mesh['ctx'=64,'head'=8] {'head'}, use_global_device_ids=true, to_apply=%region_7.8 | all-reduce | flops 128 | bytes 1024 | tf_op jit(solution)/shard_map/psum | solution.py:153
  186.0 10.7 %all-gather.3 = f32[8,1,128]{2,1,0:T(1,128)S(1)} all-gather(f32[1,1,128]{2,1,0:T(1,128)S(1)} %bitcast.212), channel_id=3, replica_groups=mesh['ctx'=64,'head'=8] {'head'}, dimensions={0}, use_global_device_ids=true | all-gather | bytes 4608 | tf_op jit(solution)/shard_map/all_gather | solution.py:122
  197.6 1.0 convolution_convert_fusion
  200.2 1.3 collective-permute-start.3
  202.0 1.3 collective-permute-start.2
  203.4 2.9 collective-permute-done.3
  208.5 200.3 %all-gather.9.cloned.1.call-done = bf16[128,273,128]{2,1,0:T(8,128)(2,1)} async-done(((bf16[2,273,128]{2,1,0:T(8,128)(2,1)}), bf16[128,273,128]{2,1,0:T(8,128)(2,1)}) %all-gather.9.cloned.1.call-update) | async-done | bytes 8945680 | tf_op jit(solution)/shard_map/all_gather | solution.py:25
  408.8 61.5 %while.23 = (s32[]{:T(128)}, f32[2,273,128]{2,1,0:T(8,128)S(1)}, s32[]{:T(128)}, bf16[64,2,273,128]{3,2,1,0:T(8,128)(2,1)}, s32[]{:T(128)}, /*index=5*/s32[]{:T(128)}, s32[]{:T(128)}, s32[]{:T(128)}) while((s32[]{:T(128)}, f32[2,273,128]{2,1,0:T(8,128)S(1)}, s32[]{:T(128)}, bf16[64,2,273,128]{3,2,1,0:T(8,128)(2,1)}, s32[]{:T(128)}, ...), condition=%wide.region_11.12_spmd, body=%wide.region_10.11_spmd.sunk | while | flops 139782 | bytes 699023 | solution.py:32
  408.9 1.0 convert_add_fusion.5
  409.8 1.0 convert_add_fusion.5
  410.8 1.0 convert_add_fusion.5
  411.8 1.0 convert_add_fusion.5
  412.8 1.0 convert_add_fusion.5
  413.8 1.0 convert_add_fusion.5
  414.7 1.0 convert_add_fusion.5
  415.7 1.0 convert_add_fusion.5
  416.7 1.0 convert_add_fusion.5
  417.7 1.0 convert_add_fusion.5
  418.6 1.0 convert_add_fusion.5
  419.6 1.0 convert_add_fusion.5
  420.6 1.0 convert_add_fusion.5
  421.6 1.0 convert_add_fusion.5
  422.5 1.0 convert_add_fusion.5
  423.5 1.0 convert_add_fusion.5
  424.5 1.0 convert_add_fusion.5
  425.5 1.0 convert_add_fusion.5
  426.5 1.0 convert_add_fusion.5
  427.4 1.0 convert_add_fusion.5
  428.4 1.0 convert_add_fusion.5
  429.4 1.0 convert_add_fusion.5
  430.4 1.0 convert_add_fusion.5
  431.3 1.0 convert_add_fusion.5
  432.3 1.0 convert_add_fusion.5
  433.3 1.0 convert_add_fusion.5
  434.3 1.0 convert_add_fusion.5
  435.2 1.0 convert_add_fusion.5
  436.2 1.0 convert_add_fusion.5
  437.2 1.0 convert_add_fusion.5
  438.2 1.0 convert_add_fusion.5
  439.2 1.0 convert_add_fusion.5
  440.1 1.0 convert_add_fusion.5
  441.1 1.0 convert_add_fusion.5
  442.1 1.0 convert_add_fusion.5
  443.1 1.0 convert_add_fusion.5
  444.0 1.0 convert_add_fusion.5
  445.0 1.0 convert_add_fusion.5
  448.9 1.0 convert_add_fusion.5
  449.9 1.0 convert_add_fusion.5
  450.9 1.0 convert_add_fusion.5
  451.9 1.0 convert_add_fusion.5
  452.8 1.0 convert_add_fusion.5
  458.7 1.0 convert_add_fusion.5
  459.7 1.0 convert_add_fusion.5
  460.6 1.0 convert_add_fusion.5
  461.6 1.0 convert_add_fusion.5
  462.6 1.0 convert_add_fusion.5
  467.5 1.0 convert_add_fusion.5
  468.5 1.0 convert_add_fusion.5
  469.4 1.0 convert_add_fusion.5
  (91 shorter events, 27.7 us)
Async XLA Ops:
  7.2 168.3 %copy-start = (bf16[128,256]{1,0:T(8,128)(2,1)S(1)}, bf16[128,256]{1,0:T(8,128)(2,1)}, u32[]{:S(2)}) copy-start(bf16[128,256]{1,0:T(8,128)(2,1)} %param.13) | copy-start | bytes 196612
  7.2 168.7 %copy-start.1 = (bf16[128,256]{1,0:T(8,128)(2,1)S(1)}, bf16[128,256]{1,0:T(8,128)(2,1)}, u32[]{:S(2)}) copy-start(bf16[128,256]{1,0:T(8,128)(2,1)} %param.17) | copy-start | bytes 196612
  7.2 168.7 %copy-start.4 = (f32[256]{0:T(256)S(1)}, f32[256]{0:T(256)}, u32[]{:S(2)}) copy-start(f32[256]{0:T(256)} %param.16) | copy-start | bytes 3076
  7.2 167.9 %all-gather.7.cloned.1.call-start = ((), (), s32[]{:S(2)}) async-start(), calls=%async_computation | async-start | bytes 9318400 | tf_op jit(solution)/shard_map/all_gather | solution.py:25
  10.5 398.3 %all-gather.9.cloned.1.call-start = ((), (), s32[]{:S(2)}) async-start(), calls=%async_computation.1 | async-start | bytes 9318400 | tf_op jit(solution)/shard_map/all_gather | solution.py:25
  10.6 13.6 %collective-permute-start = (bf16[128,256]{1,0:T(8,128)(2,1)}, bf16[128,256]{1,0:T(8,128)(2,1)S(1)}, u32[]{:S(2)}, u32[]{:S(2)}) collective-permute-start(bf16[128,256]{1,0:T(8,128)(2,1)} %param.13), channel_id=1, source_target_pairs={{0,8},{8,16},{16,24},{24,32},{32,40},{40,48},{48,56},{56,64},{64,7... | collective-permute-start | bytes 196616 | tf_op jit(solution)/shard_map/ppermute | solution.py:18
  15.0 9.0 %collective-permute-start.1 = (bf16[128,256]{0,1:T(8,128)(2,1)S(1)}, bf16[128,256]{0,1:T(8,128)(2,1)S(1)}, u32[]{:S(2)}, u32[]{:S(2)}) collective-permute-start(bf16[128,256]{0,1:T(8,128)(2,1)S(1)} %copy.83), channel_id=1, source_target_pairs={{0,8},{8,16},{16,24},{24,32},{32,40},{40,48},{48,56},{56,64},{64,7... | collective-permute-start | bytes 196616 | tf_op jit(solution)/shard_map/ppermute | solution.py:18
  24.3 183.4 %copy-start.2 = (bf16[128,32]{0,1:T(8,128)(2,1)S(1)}, bf16[128,32]{0,1:T(8,128)(2,1)}, u32[]{:S(2)}) copy-start(bf16[128,32]{0,1:T(8,128)(2,1)} %param.12) | copy-start | bytes 24580
  175.1 296.1 %copy-start.3 = (bf16[128,32]{0,1:T(8,128)(2,1)S(1)}, bf16[128,32]{0,1:T(8,128)(2,1)}, u32[]{:S(2)}) copy-start(bf16[128,32]{0,1:T(8,128)(2,1)} %param.11) | copy-start | bytes 24580
  200.2 6.2 %collective-permute-start.3 = (bf16[128,256]{0,1:T(8,128)(2,1)S(1)}, bf16[128,256]{0,1:T(8,128)(2,1)S(1)}, u32[]{:S(2)}, u32[]{:S(2)}) collective-permute-start(bf16[128,256]{0,1:T(8,128)(2,1)S(1)} %bitcast.206), channel_id=1, source_target_pairs={{8,0},{16,8},{24,16},{32,24},{40,32},{48,40},{56,48},{64,56},{72,6... | collective-permute-start | bytes 196616 | tf_op jit(solution)/shard_map/ppermute | solution.py:18
  202.0 270.1 %collective-permute-start.2 = (bf16[128,256]{1,0:T(8,128)(2,1)S(1)}, bf16[128,256]{1,0:T(8,128)(2,1)S(1)}, u32[]{:S(2)}, u32[]{:S(2)}) collective-permute-start(bf16[128,256]{1,0:T(8,128)(2,1)S(1)} %copy.99), channel_id=1, source_target_pairs={{8,0},{16,8},{24,16},{32,24},{40,32},{48,40},{56,48},{64,56},{72,6... | collective-permute-start | bytes 196616 | tf_op jit(solution)/shard_map/ppermute | solution.py:18
Sparse Core Ops, SparseCore 0:
  11.0 164.0 all-gather.6
  198.7 210.0 all-gather.8
